TPU v7x, 256 devices: a whole 4x4x8 slice. The times are simulated.
256 devices in a mesh: req: 32 (over z_lo, x, core), tp: 8 (over z_hi, y).
Axes of the slice: x: 4, y: 4, z: 8 (z_hi: 2, z_lo: 4; z = z_hi * 4 + z_lo), core: 2. Of those that a mesh axis runs over, the one named last changes fastest.
Arguments:
- hidden: bfloat16 [8192, 4608], P('req', 'tp'), may hold values from -6 to 6
- norm_gain: float32 [4608], replicated, may hold values from 0.1 to 1.9
- w_query: bfloat16 [4608, 4096], P(None, 'tp'), may hold values from -0.25 to 0.25
- w_key: bfloat16 [4608, 2048], P(None, 'tp'), may hold values from -0.09375 to 0.09375
- w_value: bfloat16 [4608, 2048], P(None, 'tp'), may hold values from -0.09375 to 0.09375
- prefix_kv: bfloat16 [16384, 2, 2048], P('req', None, 'tp'), may hold values from -6 to 6
- group_of: int32 [32], replicated, may hold values from 0 to 3, as said below
- block_owner: int32 [4, 8], replicated, may hold values from 0 to 31, as said below
- lengths: int32 [32], replicated, may hold values from 32 to 256, as said below
Outputs:
- attended: bfloat16 [8192, 4096], P('req', 'tp')
- key_cache: bfloat16 [8192, 2048], P('req', 'tp')
- value_cache: bfloat16 [8192, 2048], P('req', 'tp')
Inputs may be any that keep to these rules, and one draw needn't show every extreme that they name: `group_of`: every group holds exactly 8 requests. `block_owner`: every block index appears exactly once. `lengths`: some request has exactly 256 live rows and some exactly 32.
All inputs are finite; a program needn't handle non-finite values.
Results may differ from a plain program's by a relative error of at most 0.011.
Values may be sent and summed in bfloat16 or wider, within the bound.
A program may use at most 256 MiB of HBM per device.

v0:
```python
import math
import jax
import jax.numpy as jnp
from jax import lax
from jax.sharding import PartitionSpec as P

HD = 128
GSIZE = 8
PREFIX = 4096
SOFTCAP = 50.0
EPSILON = 1e-06
QUERY_SCALE = 1.0 / 12.0


def rope_tables(positions, head_width):
    half_width = head_width // 2
    inverse_freq = jnp.exp(
        jnp.arange(half_width).astype(jnp.float32) * (-2.0 * math.log(10000.0) / head_width)
    )
    angles = positions.astype(jnp.float32)[:, None] * inverse_freq[None, :]
    return (jnp.cos(angles), jnp.sin(angles))


def rotate(values, cosine_table, sine_table):
    half_width = values.shape[-1] // 2
    lower_half = values[..., :half_width]
    upper_half = values[..., half_width:]
    cosine_part = cosine_table[:, None, :]
    sine_part = sine_table[:, None, :]
    return jnp.concatenate(
        [
            lower_half * cosine_part - upper_half * sine_part,
            upper_half * cosine_part + lower_half * sine_part,
        ],
        axis=-1,
    )


def attend(grouped, key_block, value_block, allowed_mask):
    scores = jnp.einsum("rkgd,ckd->kgrc", grouped, key_block, preferred_element_type=jnp.float32)
    weights = jnp.exp(SOFTCAP * jnp.tanh(scores / SOFTCAP))
    if allowed_mask is not None:
        weights = jnp.where(allowed_mask[None, None], weights, 0.0)
    denominator = jnp.transpose(jnp.sum(weights, axis=3), (2, 0, 1))
    numerator = jnp.einsum(
        "kgrc,ckd->rkgd",
        weights.astype(jnp.bfloat16),
        value_block,
        preferred_element_type=jnp.float32,
    )
    return (numerator, denominator)


def body(hidden, norm_gain, w_query, w_key, w_value, prefix_kv, group_of, block_owner, lengths):
    device = lax.axis_index("req")
    row_count = hidden.shape[0]
    gathered = lax.all_gather(hidden, "tp", axis=1, tiled=True)
    features = gathered.astype(jnp.float32)
    row_scale = lax.rsqrt(jnp.mean(features * features, axis=1, keepdims=True) + EPSILON)
    normed = (features * row_scale * norm_gain[None, :]).astype(jnp.bfloat16)
    heads_query = w_query.shape[1] // HD
    heads_kv = w_key.shape[1] // HD
    group_size = heads_query // heads_kv
    query_raw = jnp.dot(normed, w_query, preferred_element_type=jnp.float32)
    key_raw = jnp.dot(normed, w_key, preferred_element_type=jnp.float32)
    value_raw = jnp.dot(normed, w_value, preferred_element_type=jnp.float32)
    cosine_table, sine_table = rope_tables(jnp.arange(row_count) + PREFIX, HD)
    query_rows = (
        rotate(query_raw.reshape(row_count, heads_query, HD), cosine_table, sine_table)
        * QUERY_SCALE
    ).astype(jnp.bfloat16)
    live_rows = jnp.arange(row_count) < lengths[device]
    key_rows = jnp.where(
        live_rows[:, None, None],
        rotate(key_raw.reshape(row_count, heads_kv, HD), cosine_table, sine_table),
        0.0,
    ).astype(jnp.bfloat16)
    value_rows = jnp.where(live_rows[:, None], value_raw, 0.0).astype(jnp.bfloat16)
    grouped = query_rows.reshape(row_count, heads_kv, group_size, HD)
    causal = jnp.arange(row_count)[:, None] >= jnp.arange(row_count)[None, :]
    numerator, denominator = attend(
        grouped, key_rows, value_rows.reshape(row_count, heads_kv, HD), causal
    )
    device_count = lax.axis_size("req")
    flat_query = query_rows.reshape(row_count, heads_query * HD)
    everyone = lax.all_gather(flat_query, "req", axis=0, tiled=True)
    owned_group = jnp.sum(
        jnp.any(block_owner == device, axis=1).astype(jnp.int32)
        * jnp.arange(block_owner.shape[0], dtype=jnp.int32)
    )
    members = jnp.argsort((group_of != owned_group).astype(jnp.int32), stable=True)[:GSIZE]
    chosen = everyone.reshape(device_count, row_count, heads_kv, group_size, HD)[members]
    block_count = prefix_kv.shape[0]
    key_block = prefix_kv[:, 0].reshape(block_count, heads_kv, HD)
    value_block = prefix_kv[:, 1].reshape(block_count, heads_kv, HD)
    extra_num, extra_den = attend(
        chosen.reshape(GSIZE * row_count, heads_kv, group_size, HD), key_block, value_block, None
    )
    full_num = jnp.zeros((device_count, row_count, heads_kv * group_size * HD), jnp.float32)
    full_num = full_num.at[members].set(
        extra_num.reshape(GSIZE, row_count, heads_kv * group_size * HD)
    )
    full_den = jnp.zeros((device_count, row_count, heads_kv * group_size), jnp.float32)
    full_den = full_den.at[members].set(extra_den.reshape(GSIZE, row_count, heads_kv * group_size))
    got_num, got_den = (
        lax.psum_scatter(
            full_num.reshape(device_count * row_count, -1), "req", scatter_dimension=0, tiled=True
        ),
        lax.psum_scatter(
            full_den.reshape(device_count * row_count, -1), "req", scatter_dimension=0, tiled=True
        ),
    )
    numerator = numerator + got_num.reshape(numerator.shape)
    denominator = denominator + got_den.reshape(denominator.shape)
    attended = numerator / denominator[..., None]
    attended = jnp.where(live_rows[:, None, None, None], attended, 0.0).astype(jnp.bfloat16)
    return (
        attended.reshape(row_count, heads_query * HD),
        key_rows.reshape(row_count, heads_kv * HD),
        value_rows,
    )


def solution(mesh):
    in_specs = (
        P("req", "tp"),
        P(),
        P(None, "tp"),
        P(None, "tp"),
        P(None, "tp"),
        P("req", None, "tp"),
        P(),
        P(),
        P(),
    )
    out_specs = (P("req", "tp"), P("req", "tp"), P("req", "tp"))
    return jax.shard_map(body, mesh=mesh, in_specs=in_specs, out_specs=out_specs, check_vma=False)
```

profile of v0, /device:TPU:8, one launch (start us, length us, event | category | flops | bytes accessed | tf_op | source)
XLA Modules:
  0.0 566.9 jit_solution(6024013331039307176)
XLA Ops:
  9.2 84.1 %all-gather.3.cloned.1.call-done = bf16[256,4608]{0,1:T(8,128)(2,1)} async-done(((bf16[256,576]{0,1:T(8,128)(2,1)}), bf16[256,4608]{0,1:T(8,128)(2,1)}) %all-gather.3.cloned.1.call-update) | async-done | bytes 2359312 | tf_op jit(solution)/shard_map/all_gather | solution.py:57
  93.3 2.3 fusion.1
  95.6 5.6 fusion.30
  106.4 1.8 copy.106
  108.4 1.8 fusion.35
  110.2 1.9 copy.141
  116.4 73.9 %all-gather.5.cloned.1.call-done = bf16[8192,512]{0,1:T(8,128)(2,1)} async-done(((bf16[256,512]{0,1:T(8,128)(2,1)}), bf16[8192,512]{0,1:T(8,128)(2,1)}) %all-gather.5.cloned.1.call-update) | async-done | bytes 8388624 | tf_op jit(solution)/shard_map/all_gather | solution.py:86
  190.3 9.5 %copy.143 = bf16[64,8,32,256]{3,2,1,0:T(8,128)(2,1)} copy(bf16[64,8,32,256]{3,1,2,0:T(8,128)(2,1)} %bitcast.85) | data formatting | bytes 16777216
  199.9 14.6 %copy.107 = bf16[32,256,2,2,128]{4,1,3,2,0:T(8,128)(2,1)} copy(bf16[32,256,2,2,128]{1,0,4,3,2:T(8,128)(2,1)} %bitcast.83) | data formatting | bytes 16777216 | tf_op jit(solution)/shard_map/reshape | solution.py:92
  214.5 5.6 gather_fusion
  220.1 1.8 copy.108
  221.9 9.2 %bitcast_reduce_fusion = (f32[2,2,2048]{2,1,0:T(2,128)S(1)}, f32[2,2048,2,512]{1,3,2,0:T(8,128)}) fusion(bf16[2048,2,2,128]{3,0,2,1:T(8,128)(2,1)S(1)} %bitcast.86, bf16[512,2,128,1]{0,2,3,1:T(8,128)(2,1)} %bitcast.92), kind=kOutput, calls=%fused_computation.3 | convolution fusion | flops 1086316544 | bytes 19169280 | tf_op jit(solution)/shard_map/rkgd,ckd->kgrc/dot_general | solution.py:40
  231.8 2.7 copy.134
  234.9 13.0 %fusion.4 = f32[2048,2,2,128]{3,0,2,1:T(8,128)} fusion(bf16[512,2,128,1]{0,2,3,1:T(8,128)(2,1)S(1)} %bitcast.90, f32[2,2048,2,512]{1,3,2,0:T(8,128)} %get-tuple-element.36), kind=kOutput, calls=%fused_computation.12 | convolution fusion | flops 1086324736 | bytes 21233664 | tf_op jit(solution)/shard_map/kgrc,ckd->rkgd/dot_general | solution.py:45
  247.8 8.7 %copy.133 = f32[2048,2,2,128]{3,2,1,0:T(2,128)} copy(f32[2048,2,2,128]{3,0,2,1:T(8,128)} %fusion.4) | data formatting | bytes 8388608 | tf_op jit(solution)/shard_map/reshape | solution.py:101
  256.6 6.4 %reshape.187 = f32[8,256,512]{2,1,0:T(8,128)} reshape(f32[2048,2,2,128]{3,2,1,0:T(2,128)} %copy.133) | data formatting | bytes 8388608 | tf_op jit(solution)/shard_map/reshape | solution.py:101
  263.0 7.9 %broadcast_in_dim.81 = f32[32,256,512]{2,1,0:T(8,128)} broadcast(f32[]{:T(128)} %constant.6.clone.1), dimensions={} | broadcast | bytes 16777220 | tf_op jit(solution)/shard_map/broadcast_in_dim | solution.py:99
  270.9 8.0 %scatter_fusion = f32[32,256,512]{2,1,0:T(8,128)} fusion(f32[32,256,512]{2,1,0:T(8,128)} %broadcast_in_dim.81, s32[8]{0:T(128)S(1)} %compare_select_fusion, f32[8,256,512]{2,1,0:T(8,128)} %reshape.187), kind=kCustom, calls=%fused_computation.1 | custom fusion | bytes 12582944 | tf_op jit(solution)/shard_map/scatter | solution.py:100
  278.9 17.5 %copy.116 = f32[8192,512]{0,1:T(8,128)} copy(f32[8192,512]{1,0:T(8,128)} %bitcast.82) | data formatting | bytes 33554432 | tf_op jit(solution)/shard_map/reshape | solution.py:107
  298.9 3.2 fusion.14
  303.5 4.0 fusion.32
  317.0 2.3 fusion.38
  319.2 67.6 %reduce-scatter.7.cloned.1.call-done = f32[256,4]{1,0:T(8,128)} async-done(((f32[8192,4]{1,0:T(8,128)}), f32[256,4]{1,0:T(8,128)}) %reduce-scatter.7.cloned.1.call-update) | async-done | bytes 4112
  387.9 170.1 %reduce-scatter.5.cloned.1.call-done = f32[256,512]{0,1:T(8,128)} async-done(((f32[8192,512]{0,1:T(8,128)}), f32[256,512]{0,1:T(8,128)}) %reduce-scatter.5.cloned.1.call-update) | async-done | bytes 524304 | tf_op jit(solution)/shard_map/reduce_scatter | solution.py:106
  (64 shorter events, 29.4 us)
Async XLA Ops:
  7.2 291.8 %copy-start = (bf16[4608,256]{1,0:T(8,128)(2,1)S(1)}, bf16[4608,256]{1,0:T(8,128)(2,1)}, u32[]{:S(2)}) copy-start(bf16[4608,256]{1,0:T(8,128)(2,1)} %param.13) | copy-start | bytes 7077892
  7.2 86.1 %all-gather.3.cloned.1.call-start = ((), (), s32[]{:S(2)}) async-start(), calls=%async_computation.2 | async-start | bytes 2654208 | tf_op jit(solution)/shard_map/all_gather | solution.py:57
  7.9 182.4 %all-gather.5.cloned.1.call-start = ((), (), s32[]{:S(2)}) async-start(), calls=%async_computation.3 | async-start | bytes 8650752 | tf_op jit(solution)/shard_map/all_gather | solution.py:86
  101.2 7.2 %copy-start.1 = (bf16[512,2,256]{2,1,0:T(2,128)(2,1)S(1)}, bf16[512,2,256]{2,1,0:T(2,128)(2,1)}, u32[]{:S(2)}) copy-start(bf16[512,2,256]{2,1,0:T(2,128)(2,1)} %param.14) | copy-start | bytes 1572868
  101.2 12.1 %copy-start.5 = (s32[4,8]{1,0:T(4,128)S(1)}, s32[4,8]{1,0:T(4,128)}, u32[]{:S(2)}) copy-start(s32[4,8]{1,0:T(4,128)} %param.16) | copy-start | bytes 388
  101.2 12.9 %copy-start.7 = (s32[32]{0:T(128)S(1)}, s32[32]{0:T(128)}, u32[]{:S(2)}) copy-start(s32[32]{0:T(128)} %param.15) | copy-start | bytes 388
  104.6 0.8 copy-start.2
  108.2 278.7 %reduce-scatter.7.cloned.1.call-start = ((), (), s32[]{:S(2)}) async-start(), calls=%async_computation.5 | async-start | bytes 4325376
  234.6 323.4 %reduce-scatter.5.cloned.1.call-start = ((), (), s32[]{:S(2)}) async-start(), calls=%async_computation.4 | async-start | bytes 17301504 | tf_op jit(solution)/shard_map/reduce_scatter | solution.py:106
  296.4 0.7 copy-start.8
  296.4 2.5 copy-start.6
  302.1 0.6 copy-start.4
  303.5 13.4 %copy-start.3 = (f32[256,4,64]{2,0,1:T(8,128)S(1)}, f32[256,4,64]{2,0,1:T(8,128)}, u32[]{:S(2)}) copy-start(f32[256,4,64]{2,0,1:T(8,128)} %copy-done.2) | copy-start | bytes 786436
Sparse Core Ops, SparseCore 0:
  10.6 82.6 all-gather.2
  108.3 82.0 all-gather.4
  234.7 152.1 reduce-scatter.6
  389.3 168.6 reduce-scatter.4
where the time goes:
time: 568 us; the launch traced here: 567 us
  waiting for transfers between devices  397 us (70%)
  local copies, waits for them, and re-layouts  104 us (18%)
  matrix products  38.6 us (7%)
  between operations  14 us (2%)
  other arithmetic  12.9 us (2%)
    reduce_scatter x1, waiting for transfers between devices, body(): lax.psum_scatter(full_num.reshape(device_count * row_count, -1), 'req', s...  170 us
    all_gather x1, waiting for transfers between devices, body(): gathered = lax.all_gather(hidden, 'tp', axis=1, tiled=True)  84.1 us
    all_gather x1, waiting for transfers between devices, body(): everyone = lax.all_gather(flat_query, 'req', axis=0, tiled=True)  73.9 us
    unnamed x5, waiting for transfers between devices  68.4 us
    unnamed x30, local copies, waits for them, and re-layouts  27.2 us
    reshape x1, local copies, waits for them, and re-layouts, body(): full_num.reshape(device_count * row_count, -1)  17.5 us
    reshape x2, local copies, waits for them, and re-layouts, body(): extra_num.reshape(GSIZE, row_count, heads_kv * group_size * HD)  15.2 us
    reshape x1, local copies, waits for them, and re-layouts, body(): everyone.reshape(device_count, row_count, heads_kv, group_size, HD)[members]  14.6 us
  transfers between devices with their start and end apart: 4, of which 4 were waited for; matrix products, arithmetic and copies ran while one was open for 16% of the time, Pallas kernels for 0%

commit v1 on v0

--- a/solution.py
+++ b/solution.py
@@ -54,7 +54,9 @@
 def body(hidden, norm_gain, w_query, w_key, w_value, prefix_kv, group_of, block_owner, lengths):
     device = lax.axis_index("req")
     row_count = hidden.shape[0]
-    gathered = lax.all_gather(hidden, "tp", axis=1, tiled=True)
+    gathered = jnp.concatenate(
+        lax.all_to_all(jnp.stack([hidden] * lax.axis_size("tp")), "tp", 0, 0), axis=1
+    )
     features = gathered.astype(jnp.float32)
     row_scale = lax.rsqrt(jnp.mean(features * features, axis=1, keepdims=True) + EPSILON)
     normed = (features * row_scale * norm_gain[None, :]).astype(jnp.bfloat16)

time: 568 us -> 547 us (0.963)
  waiting for transfers between devices: 397 us -> 365 us
  starting transfers between devices: 0.56 us -> 11.8 us
  matrix products: 38.6 us -> 31.8 us
    all_gather x1 -> x0, waiting for transfers between devices: 84.1 us -> none  [body(): gathered = lax.all_gather(hidden, 'tp', axis=1, tiled=True)]
    all_to_all x0 -> x1, waiting for transfers between devices: none -> 33 us  [body(): lax.all_to_all(jnp.stack([hidden] * lax.axis_size('tp')), 'tp', 0, 0)]
    all_gather x1, waiting for transfers between devices: 73.9 us -> 90.6 us  [body(): everyone = lax.all_gather(flat_query, 'req', axis=0, tiled=True)]
    all_to_all x0 -> x1, starting transfers between devices: none -> 11.5 us  [body(): lax.all_to_all(jnp.stack([hidden] * lax.axis_size('tp')), 'tp', 0, 0)]
    dot_general x0 -> x2, local copies, waits for them, and re-layouts: none -> 11 us  [the longest x1 6.7 us: body(): query_raw = jnp.dot(normed, w_query, preferred_element_type=jnp.float32)]
    unnamed x30 -> x28, local copies, waits for them, and re-layouts: 27.2 us -> 19.4 us
    unnamed x5 -> x4, waiting for transfers between devices: 68.4 us -> 70.8 us
  transfers between devices with their start and end apart: 4 -> 4, of which waited for: 4 -> 4; matrix products, arithmetic and copies ran while one was open for 16% -> 18% of each run, Pallas kernels for 0% -> 0%
where the time goes in v1:
time: 547 us; the launch traced here: 545 us
  waiting for transfers between devices  365 us (67%)
  local copies, waits for them, and re-layouts  109 us (20%)
  matrix products  31.8 us (6%)
  between operations  14 us (3%)
  other arithmetic  13.3 us (2%)
  starting transfers between devices  11.8 us (2%)
    reduce_scatter x1, waiting for transfers between devices, body(): lax.psum_scatter(full_num.reshape(device_count * row_count, -1), 'req', s...  171 us
    all_gather x1, waiting for transfers between devices, body(): everyone = lax.all_gather(flat_query, 'req', axis=0, tiled=True)  90.6 us
    unnamed x4, waiting for transfers between devices  70.8 us
    all_to_all x1, waiting for transfers between devices, body(): lax.all_to_all(jnp.stack([hidden] * lax.axis_size('tp')), 'tp', 0, 0)  33 us
    unnamed x28, local copies, waits for them, and re-layouts  19.4 us
    reshape x1, local copies, waits for them, and re-layouts, body(): full_num.reshape(device_count * row_count, -1)  17.5 us
    reshape x2, local copies, waits for them, and re-layouts, body(): extra_num.reshape(GSIZE, row_count, heads_kv * group_size * HD)  15.2 us
    reshape x1, local copies, waits for them, and re-layouts, body(): everyone.reshape(device_count, row_count, heads_kv, group_size, HD)[members]  14.6 us
  transfers between devices with their start and end apart: 4, of which 4 were waited for; matrix products, arithmetic and copies ran while one was open for 18% of the time, Pallas kernels for 0%

profile of v1, /device:TPU:8, one launch (start us, length us, event | category | flops | bytes accessed | tf_op | source)
XLA Modules:
  0.0 545.5 jit_solution(9373684520356153828)
XLA Ops:
  7.2 2.7 stack.2
  9.9 11.5 %all-to-all-start = ((bf16[8,256,576]{1,2,0:T(8,128)(2,1)}), bf16[8,256,576]{1,2,0:T(8,128)(2,1)}, u32[]{:S(2)}, u32[]{:S(2)}) async-start(bf16[8,256,576]{1,2,0:T(8,128)(2,1)} %stack.2), calls=%async_computation | async-start | bytes 4718592 | tf_op jit(solution)/shard_map/all_to_all | solution.py:58
  21.5 6.7 %copy.100 = bf16[512,4608]{1,0:T(8,128)(2,1)} copy(bf16[512,4608]{0,1:T(8,128)(2,1)} %bitcast.105) | data formatting | bytes 9437184 | tf_op jit(solution)/shard_map/dot_general | solution.py:66
  28.6 33.0 %all-to-all-done = bf16[8,256,576]{1,2,0:T(8,128)(2,1)} async-done(((bf16[8,256,576]{1,2,0:T(8,128)(2,1)}), bf16[8,256,576]{1,2,0:T(8,128)(2,1)}, u32[]{:S(2)}, u32[]{:S(2)}) %all-to-all-start) | async-done | bytes 2359328 | tf_op jit(solution)/shard_map/all_to_all | solution.py:58
  61.6 2.5 multiply_reduce_fusion
  68.5 3.2 fusion.29
  77.8 90.6 %all-gather.2.cloned.1.call-done = bf16[8192,512]{0,1:T(8,128)(2,1)} async-done(((bf16[256,512]{0,1:T(8,128)(2,1)}), bf16[8192,512]{0,1:T(8,128)(2,1)}) %all-gather.2.cloned.1.call-update) | async-done | bytes 8388624 | tf_op jit(solution)/shard_map/all_gather | solution.py:88
  168.4 9.5 %copy.111 = bf16[64,8,32,256]{3,2,1,0:T(8,128)(2,1)} copy(bf16[64,8,32,256]{3,1,2,0:T(8,128)(2,1)} %bitcast.104) | data formatting | bytes 16777216
  177.9 14.6 %copy.73 = bf16[32,256,2,2,128]{4,1,3,2,0:T(8,128)(2,1)} copy(bf16[32,256,2,2,128]{1,0,4,3,2:T(8,128)(2,1)} %bitcast.102) | data formatting | bytes 16777216 | tf_op jit(solution)/shard_map/reshape | solution.py:94
  192.5 5.6 %gather_fusion = bf16[8,256,2,2,128]{4,1,3,2,0:T(8,128)(2,1)} fusion(bf16[32,256,2,2,128]{4,1,3,2,0:T(8,128)(2,1)} %copy.73, s32[1024]{0:T(1024)S(1)} %pad_clamp_fusion), kind=kCustom, calls=%fused_computation | custom fusion | bytes 4194336 | tf_op jit(solution)/shard_map/gather | solution.py:94
  199.9 9.2 %bitcast_reduce_fusion = (f32[2,2,2048]{2,1,0:T(2,128)S(1)}, f32[2,2048,2,512]{1,3,2,0:T(8,128)}) fusion(bf16[2048,2,2,128]{3,0,2,1:T(8,128)(2,1)S(1)} %bitcast.113, bf16[512,2,128,1]{0,2,3,1:T(8,128)(2,1)} %bitcast.116), kind=kOutput, calls=%fused_computation.3 | convolution fusion | flops 1086316544 | bytes 19169280 | tf_op jit(solution)/shard_map/rkgd,ckd->kgrc/dot_general | solution.py:40
  209.9 2.7 copy.106
  212.9 13.0 %fusion.3 = f32[2048,2,2,128]{3,0,2,1:T(8,128)} fusion(bf16[512,2,128,1]{0,2,3,1:T(8,128)(2,1)S(1)} %bitcast.115, f32[2,2048,2,512]{1,3,2,0:T(8,128)} %get-tuple-element.26), kind=kOutput, calls=%fused_computation.12 | convolution fusion | flops 1086324736 | bytes 21233664 | tf_op jit(solution)/shard_map/kgrc,ckd->rkgd/dot_general | solution.py:45
  225.8 8.7 %copy.105 = f32[2048,2,2,128]{3,2,1,0:T(2,128)} copy(f32[2048,2,2,128]{3,0,2,1:T(8,128)} %fusion.3) | data formatting | bytes 8388608 | tf_op jit(solution)/shard_map/reshape | solution.py:103
  234.6 6.4 %reshape.212 = f32[8,256,512]{2,1,0:T(8,128)} reshape(f32[2048,2,2,128]{3,2,1,0:T(2,128)} %copy.105) | data formatting | bytes 8388608 | tf_op jit(solution)/shard_map/reshape | solution.py:103
  241.0 7.9 %broadcast_in_dim.81 = f32[32,256,512]{2,1,0:T(8,128)} broadcast(f32[]{:T(128)} %constant.6.clone.1), dimensions={} | broadcast | bytes 16777220 | tf_op jit(solution)/shard_map/broadcast_in_dim | solution.py:101
  248.9 8.0 %scatter_fusion = f32[32,256,512]{2,1,0:T(8,128)} fusion(f32[32,256,512]{2,1,0:T(8,128)} %broadcast_in_dim.81, s32[8]{0:T(128)S(1)} %compare_select_fusion, f32[8,256,512]{2,1,0:T(8,128)} %reshape.212), kind=kCustom, calls=%fused_computation.1 | custom fusion | bytes 12582944 | tf_op jit(solution)/shard_map/scatter | solution.py:102
  256.9 17.5 %copy.82 = f32[8192,512]{0,1:T(8,128)} copy(f32[8192,512]{1,0:T(8,128)} %bitcast.101) | data formatting | bytes 33554432 | tf_op jit(solution)/shard_map/reshape | solution.py:109
  274.4 4.3 copy.96
  280.6 3.2 fusion.2
  285.8 3.2 fusion.31
  291.7 2.5 fusion.30
  294.2 70.7 %reduce-scatter.7.cloned.1.call-done = f32[256,4]{1,0:T(8,128)} async-done(((f32[8192,4]{1,0:T(8,128)}), f32[256,4]{1,0:T(8,128)}) %reduce-scatter.7.cloned.1.call-update) | async-done | bytes 4112
  365.9 170.8 %reduce-scatter.5.cloned.1.call-done = f32[256,512]{0,1:T(8,128)} async-done(((f32[8192,512]{0,1:T(8,128)}), f32[256,512]{0,1:T(8,128)}) %reduce-scatter.5.cloned.1.call-update) | async-done | bytes 524304 | tf_op jit(solution)/shard_map/reduce_scatter | solution.py:108
  (65 shorter events, 23.4 us)
Async XLA Ops:
  7.2 276.7 %copy-start = (bf16[4608,256]{1,0:T(8,128)(2,1)S(1)}, bf16[4608,256]{1,0:T(8,128)(2,1)}, u32[]{:S(2)}) copy-start(bf16[4608,256]{1,0:T(8,128)(2,1)} %param.13) | copy-start | bytes 7077892
  7.2 14.3 %copy-start.6 = (f32[4608]{0:T(1024)S(1)}, f32[4608]{0:T(1024)}, u32[]{:S(2)}) copy-start(f32[4608]{0:T(1024)} %param.10) | copy-start | bytes 55300
  9.9 51.7 %all-to-all-start = ((bf16[8,256,576]{1,2,0:T(8,128)(2,1)}), bf16[8,256,576]{1,2,0:T(8,128)(2,1)}, u32[]{:S(2)}, u32[]{:S(2)}) async-start(bf16[8,256,576]{1,2,0:T(8,128)(2,1)} %stack.2), calls=%async_computation | async-start | bytes 4718592 | tf_op jit(solution)/shard_map/all_to_all | solution.py:58
  21.4 146.9 %all-gather.2.cloned.1.call-start = ((), (), s32[]{:S(2)}) async-start(), calls=%async_computation.3 | async-start | bytes 8650752 | tf_op jit(solution)/shard_map/all_gather | solution.py:88
  61.6 4.6 copy-start.1
  66.1 1.5 copy-start.2
  67.5 7.3 %copy-start.7 = (s32[4,8]{1,0:T(4,128)S(1)}, s32[4,8]{1,0:T(4,128)}, u32[]{:S(2)}) copy-start(s32[4,8]{1,0:T(4,128)} %param.16) | copy-start | bytes 388
  67.5 8.0 %copy-start.8 = (s32[32]{0:T(128)S(1)}, s32[32]{0:T(128)}, u32[]{:S(2)}) copy-start(s32[32]{0:T(128)} %param.15) | copy-start | bytes 388
  68.4 296.5 %reduce-scatter.7.cloned.1.call-start = ((), (), s32[]{:S(2)}) async-start(), calls=%async_computation.5 | async-start | bytes 4325376
  212.6 324.0 %reduce-scatter.5.cloned.1.call-start = ((), (), s32[]{:S(2)}) async-start(), calls=%async_computation.4 | async-start | bytes 17301504 | tf_op jit(solution)/shard_map/reduce_scatter | solution.py:108
  274.4 4.3 copy-start.9
  285.0 4.0 copy-start.4
  289.0 0.6 copy-start.3
  289.6 247.0 %copy-start.5 = (bf16[256,256]{0,1:T(8,128)(2,1)S(1)}, bf16[256,256]{0,1:T(8,128)(2,1)}, u32[]{:S(2)}) copy-start(bf16[256,256]{0,1:T(8,128)(2,1)} %copy-done.4) | copy-start | bytes 393220
Sparse Core Ops, SparseCore 0:
  68.5 99.8 all-gather.1
  212.7 152.1 reduce-scatter.6
  367.5 169.1 reduce-scatter.4
